TPU v7x, 128 devices: a whole 4x4x4 slice. The times are simulated.
128 devices in a mesh: rows: 16 (over x, z_hi, core), probe: 8 (over z_lo, y).
Axes of the slice: x: 4, y: 4, z: 4 (z_hi: 2, z_lo: 2; z = z_hi * 2 + z_lo), core: 2. Of those that a mesh axis runs over, the one named last changes fastest.
Arguments:
- responses: bfloat16 [256, 131072], P('probe', 'rows'), may hold values from -6 to 6
- probes: bfloat16 [256, 131072], P('probe', 'rows'), may hold values from -6 to 6
- left_factors: bfloat16 [5, 128, 131072], P(None, None, 'rows'), may hold values from -0.5 to 0.5
- right_factors: bfloat16 [5, 128, 131072], P(None, None, 'rows'), may hold values from -0.09375 to 0.09375
- level_ranks: int32 [5], replicated, may hold values from 32 to 128, as said below
Outputs:
- basis: float32 [256, 131072], P(None, ('rows', 'probe'))
Inputs may be any that keep to these rules, and one draw needn't show every extreme that they name: `level_ranks`: some level has rank 128 and some level rank 128 // 4.
All inputs are finite; a program needn't handle non-finite values.
Results may differ from a plain program's by a relative error of at most 0.0047.
Values may be sent and summed in bfloat16 or wider, within the bound.
A program may use at most 128 MiB of HBM per device.

v0:
```python
import jax
import jax.numpy as jnp
from jax import lax
from jax.sharding import PartitionSpec as P

BLOCKS = 64


ridge_share = 0.05


def from_partner(value, axis, apart):
    mask = 2**apart
    pairs = [(source, source ^ mask) for source in range(lax.axis_size(axis))]
    return lax.ppermute(value, axis, pairs)


def shards(responses, probes, left_factors, right_factors, level_ranks):
    rows_count = lax.axis_size("rows")
    local_probes, rows_dev = responses.shape
    levels_count, rank_width, _ = left_factors.shape
    rank_iota = jnp.arange(rank_width)
    partials = []
    layouts = []
    for level_index in range(levels_count):
        clusters = 2 ** (level_index + 1)
        per_device = max(1, clusters // rows_count)
        cluster_span = max(1, rows_count // clusters)
        layouts.append((clusters, per_device, cluster_span))
        right_part = right_factors[level_index].reshape(
            rank_width, per_device, rows_dev // per_device
        )
        probe_part = probes.reshape(local_probes, per_device, rows_dev // per_device)
        partials.append(
            jnp.einsum("kcn,rcn->ckr", right_part, probe_part, preferred_element_type=jnp.float32)
        )
    siblings = []
    running = list(partials)
    finished = [None] * levels_count
    span_list = []
    for level_index in range(levels_count):
        clusters, per_device, cluster_span = layouts[level_index]
        span_list.append(cluster_span.bit_length() - 1)
        if clusters > rows_count:
            swapped = partials[level_index].reshape(per_device // 2, 2, rank_width, local_probes)[
                :, ::-1
            ]
            finished[level_index] = swapped.reshape(per_device, rank_width, local_probes)
    for bit_number in range(rows_count.bit_length() - 1):
        crossing = [
            level_index
            for level_index in range(levels_count)
            if finished[level_index] is None and span_list[level_index] >= bit_number
        ]
        payload = jnp.concatenate([running[level_index] for level_index in crossing], 0)
        received = from_partner(payload, "rows", bit_number)
        for slot_number, level_index in enumerate(crossing):
            incoming = received[slot_number : slot_number + 1]
            if span_list[level_index] > bit_number:
                running[level_index] = running[level_index] + incoming
            else:
                finished[level_index] = incoming
    siblings = finished
    residual = responses.astype(jnp.float32)
    for level_index in range(levels_count):
        clusters, per_device, cluster_span = layouts[level_index]
        keep_rows = rank_iota[None, :, None] < level_ranks[level_index]
        sibling = jnp.where(keep_rows, siblings[level_index], 0.0).astype(jnp.bfloat16)
        left_part = left_factors[level_index].reshape(
            rank_width, per_device, rows_dev // per_device
        )
        update = jnp.einsum("ckr,kcn->rcn", sibling, left_part, preferred_element_type=jnp.float32)
        residual = residual - update.reshape(local_probes, rows_dev)
    sample = residual.astype(jnp.bfloat16)
    slab = lax.all_to_all(sample, "probe", split_axis=1, concat_axis=0, tiled=True)
    all_probes, slab_rows = slab.shape
    block_rows = rows_dev * rows_count // BLOCKS
    piece_rows = min(block_rows, slab_rows)
    piece_count = slab_rows // piece_rows
    piece_view = slab.reshape(all_probes, piece_count, piece_rows)
    piece_gram = jnp.einsum(
        "rpg,spg->prs", piece_view, piece_view, preferred_element_type=jnp.float32
    )
    group_size = max(1, block_rows // slab_rows)
    full_gram = piece_gram
    bit_number = 0
    full_gram = full_gram + from_partner(full_gram, "probe", bit_number)
    shifted = full_gram + ridge_share * block_rows * jnp.eye(all_probes, dtype=jnp.float32)
    lower_factor = jnp.linalg.cholesky(shifted)
    right_sides = jnp.transpose(piece_view, (1, 0, 2)).astype(jnp.float32)
    solved = lax.linalg.triangular_solve(lower_factor, right_sides, left_side=True, lower=True)
    return jnp.transpose(solved, (1, 0, 2)).reshape(all_probes, slab_rows)


def solution(mesh):
    return jax.shard_map(
        shards,
        mesh=mesh,
        in_specs=(
            P("probe", "rows"),
            P("probe", "rows"),
            P(None, None, "rows"),
            P(None, None, "rows"),
            P(),
        ),
        out_specs=P(None, ("rows", "probe")),
        check_vma=False,
    )
```

profile of v0, /device:TPU:10, one launch (start us, length us, event | category | flops | bytes accessed | tf_op | source)
XLA Modules:
  0.0 131.9 jit_solution(17608333133139522478)
XLA Ops:
  0.0 0.0 copy-start.3
  0.0 2.5 %fusion.29 = f32[1,128,32]{1,2,0:T(8,128)S(1)} fusion(bf16[32,8192]{1,0:T(8,128)(2,1)} %param.6, bf16[5,128,8192]{2,1,0:T(8,128)(2,1)} %param.8), kind=kOutput, calls=%fused_computation.40 | convolution fusion | flops 67108864 | bytes 2637824 | tf_op jit(solution)/shard_map/kcn,rcn->ckr/dot_general | solution.py:35
  2.5 0.0 copy-done.3
  2.6 2.4 %fusion.38 = f32[1,128,32]{1,2,0:T(8,128)S(1)} fusion(bf16[32,8192]{1,0:T(8,128)(2,1)S(1)} %copy-done.3, bf16[5,128,8192]{2,1,0:T(8,128)(2,1)} %param.8), kind=kOutput, calls=%fused_computation.43 | convolution fusion | flops 67108864 | bytes 2637824 | tf_op jit(solution)/shard_map/kcn,rcn->ckr/dot_general | solution.py:35
  5.0 2.4 %fusion.35 = f32[1,128,32]{1,2,0:T(8,128)S(1)} fusion(bf16[32,8192]{1,0:T(8,128)(2,1)S(1)} %copy-done.3, bf16[5,128,8192]{2,1,0:T(8,128)(2,1)} %param.8), kind=kOutput, calls=%fused_computation.42 | convolution fusion | flops 67108864 | bytes 2637824 | tf_op jit(solution)/shard_map/kcn,rcn->ckr/dot_general | solution.py:35
  7.4 2.4 %fusion.32 = f32[1,128,32]{1,2,0:T(8,128)S(1)} fusion(bf16[32,8192]{1,0:T(8,128)(2,1)S(1)} %copy-done.3, bf16[5,128,8192]{2,1,0:T(8,128)(2,1)} %param.8), kind=kOutput, calls=%fused_computation.41 | convolution fusion | flops 67108864 | bytes 2637824 | tf_op jit(solution)/shard_map/kcn,rcn->ckr/dot_general | solution.py:35
  9.8 0.0 slice-start.1
  9.9 0.1 collective-permute-start
  10.0 1.5 %slice-done.1 = bf16[1,128,8192]{2,1,0:T(8,128)(2,1)S(1)} async-done(((bf16[5,128,8192]{2,1,0:T(8,128)(2,1)}), bf16[1,128,8192]{2,1,0:T(8,128)(2,1)S(1)}, s32[]{:S(2)}) %slice-start.1) | async-done | bytes 2097176 | tf_op jit(solution)/shard_map/slice | solution.py:30
  11.4 2.8 %reshape_squeeze.4 = bf16[128,2,4096]{2,1,0:T(2,128)(2,1)} reshape(bf16[1,128,8192]{2,1,0:T(8,128)(2,1)S(1)} %slice-done.1) | data formatting | bytes 4194304 | tf_op jit(solution)/shard_map/reshape;squeeze | solution.py:30
  14.2 0.0 copy-done.2
  14.2 0.7 fusion.71
  14.9 0.6 iota_compare_fusion.4
  15.5 0.0 slice-start
  15.5 1.6 %slice-done = bf16[1,128,8192]{2,1,0:T(8,128)(2,1)S(1)} async-done(((bf16[5,128,8192]{2,1,0:T(8,128)(2,1)}), bf16[1,128,8192]{2,1,0:T(8,128)(2,1)S(1)}, s32[]{:S(2)}) %slice-start) | async-done | bytes 2097176 | tf_op jit(solution)/shard_map/slice | solution.py:69
  17.1 2.4 %copy.29 = bf16[1,128,8192]{1,2,0:T(8,128)(2,1)} copy(bf16[1,128,8192]{2,1,0:T(8,128)(2,1)S(1)} %slice-done) | data formatting | bytes 4194304
  19.5 0.8 iota_compare_fusion.7
  20.4 2.9 %fusion.16 = bf16[2,128,32]{1,2,0:T(8,128)(2,1)S(1)} fusion(bf16[128,2,4096]{2,1,0:T(2,128)(2,1)} %reshape_squeeze.4, bf16[4,2,8,4096]{3,2,1,0:T(8,128)(2,1)S(1)} %bitcast.151), kind=kOutput, calls=%fused_computation.23 | convolution fusion | flops 67108864 | bytes 2637824 | tf_op jit(solution)/shard_map/kcn,rcn->ckr/dot_general | solution.py:35
  23.2 0.0 copy-done
  23.3 0.8 convolution_bitcast_fusion
  24.1 0.6 iota_compare_fusion.8
  24.6 0.0 collective-permute-done
  24.7 4.0 %collective-permute-start.1 = (f32[3,128,32]{1,2,0:T(8,128)S(1)}, f32[3,128,32]{1,2,0:T(8,128)S(1)}, u32[]{:S(2)}, u32[]{:S(2)}) collective-permute-start(f32[3,128,32]{1,2,0:T(8,128)S(1)} %pad_maximum_fusion.1), channel_id=1, source_target_pairs={{0,16},{8,24},{16,0},{24,8},{32,48},{40,56},{48,32},{56,40},{64,80... | collective-permute-start | bytes 147464 | tf_op jit(solution)/shard_map/ppermute | solution.py:15
  28.6 0.6 iota_compare_fusion.6
  29.3 1.4 %collective-permute-done.1 = f32[3,128,32]{1,2,0:T(8,128)S(1)} collective-permute-done((f32[3,128,32]{1,2,0:T(8,128)S(1)}, f32[3,128,32]{1,2,0:T(8,128)S(1)}, u32[]{:S(2)}, u32[]{:S(2)}) %collective-permute-start.1) | collective-permute-done | bytes 49184 | tf_op jit(solution)/shard_map/ppermute | solution.py:15
  30.7 0.6 collective-permute-start.2
  31.3 0.6 iota_compare_fusion.5
  32.0 0.1 copy.32
  32.1 0.0 copy-start.1
  32.1 2.6 %collective-permute-done.2 = f32[2,128,32]{1,2,0:T(8,128)S(1)} collective-permute-done((f32[2,128,32]{1,2,0:T(8,128)S(1)}, f32[2,128,32]{1,2,0:T(8,128)S(1)}, u32[]{:S(2)}, u32[]{:S(2)}) %collective-permute-start.2) | collective-permute-done | bytes 32800 | tf_op jit(solution)/shard_map/ppermute | solution.py:15
  34.7 2.2 %collective-permute-start.3 = (bf16[1,128,32]{1,2,0:T(8,128)(2,1)S(1)}, bf16[1,128,32]{1,2,0:T(8,128)(2,1)S(1)}, u32[]{:S(2)}, u32[]{:S(2)}) collective-permute-start(bf16[1,128,32]{1,2,0:T(8,128)(2,1)S(1)} %slice_add_fusion), channel_id=1, source_target_pairs={{0,64},{8,72},{16,80},{24,88},{32,96},{40,104},{48,112},{56,120},{... | collective-permute-start | bytes 24584 | tf_op jit(solution)/shard_map/ppermute | solution.py:15
  36.9 2.0 %fusion.5 = f32[32,8192]{1,0:T(8,128)S(1)} fusion(bf16[5,128,8192]{2,1,0:T(8,128)(2,1)} %param.7, f32[2,128,32]{1,2,0:T(8,128)S(1)} %collective-permute-done.2, pred[128]{0:T(512)(128)(4,1)S(1)} %iota_compare_fusion.7), kind=kOutput, calls=%fused_computation.12 | convolution fusion | flops 67112960 | bytes 3154432 | tf_op jit(solution)/shard_map/ckr,kcn->rcn/dot_general | solution.py:72
  38.9 0.9 collective-permute-done.3
  39.9 0.0 copy-done.1
  39.9 2.0 %fusion.1 = f32[32,8192]{1,0:T(8,128)S(1)} fusion(f32[32,8192]{1,0:T(8,128)S(1)} %fusion.5, bf16[5,128,8192]{2,1,0:T(8,128)(2,1)} %param.7, bf16[32,8192]{1,0:T(8,128)(2,1)S(1)} %copy-done.1, bf16[1,128,32]{1,2,0:T(8,128)(2,1)S(1)} %collective-permute-done.3, pred[128]{0:T(512)(128)(4,1)S(1)} %iota_compare_fusion.8), kind=kOutput, calls=%fused_computation.7 | convolution fusion | flops 67899392 | bytes 4726912 | tf_op jit(solution)/shard_map/ckr,kcn->rcn/dot_general | solution.py:72
  41.9 2.0 %convolution_subtract_fusion.1 = f32[32,8192]{1,0:T(8,128)S(1)} fusion(f32[32,8192]{1,0:T(8,128)S(1)} %fusion.1, bf16[5,128,8192]{2,1,0:T(8,128)(2,1)} %param.7, f32[3,128,32]{1,2,0:T(8,128)S(1)} %collective-permute-done.1, pred[128]{0:T(512)(128)(4,1)S(1)} %iota_compare_fusion.6), kind=kOutput, calls=%fused_computation.5 | convolution fusion | flops 67375104 | bytes 4203008 | tf_op jit(solution)/shard_map/ckr,kcn->rcn/dot_general | solution.py:72
  44.0 2.0 %fusion.2 = bf16[32,8192]{1,0:T(8,128)(2,1)S(1)} fusion(f32[32,8192]{1,0:T(8,128)S(1)} %bitcast.148, f32[32,8192]{1,0:T(8,128)S(1)} %convolution_subtract_fusion.1, bf16[5,128,8192]{2,1,0:T(8,128)(2,1)} %param.7, f32[4,128,32]{1,2,0:T(8,128)S(1)} %collective-permute-done, pred[128]{0:T(512)(128)(4,1)S(1)} %iota_compare_fusion.5), kind=kOutput, calls=%fused_computation.8 | convolution fusion | flops 67899392 | bytes 4727296 | tf_op jit(solution)/shard_map/ckr,kcn->rcn/dot_general | solution.py:72
  46.0 15.4 %all_to_all.16 = bf16[32,8,1024]{2,0,1:T(8,128)(2,1)S(1)} all-to-all(bf16[32,8,1024]{2,0,1:T(8,128)(2,1)S(1)} %bitcast.150), channel_id=1, replica_groups=mesh['rows'=16,'probe'=8] {'probe'}, dimensions={1} | all-to-all | bytes 1048576 | tf_op jit(solution)/shard_map/all_to_all | solution.py:75
  61.4 0.3 convolution_bitcast_fusion.3
  61.8 0.3 collective-permute-start.4
  62.0 6.3 %collective-permute-done.4 = f32[1,256,256]{1,2,0:T(8,128)S(1)} collective-permute-done((f32[1,256,256]{1,2,0:T(8,128)S(1)}, f32[1,256,256]{1,2,0:T(8,128)S(1)}, u32[]{:S(2)}, u32[]{:S(2)}) %collective-permute-start.4) | collective-permute-done | bytes 262176 | tf_op jit(solution)/shard_map/ppermute | solution.py:15
  68.4 0.1 copy.19
  68.6 11.7 %custom-call.16 = f32[1,128,128]{2,1,0:T(8,128)S(1)} custom-call(f32[1,128,128]{2,1,0:T(8,128)S(1)} %cholesky.114), custom_call_target="Cholesky" | custom-call | tf_op jit(solution)/shard_map/jit(cholesky)/cholesky | solution.py:89
  80.3 0.1 copy.20
  80.5 9.8 %custom-call.17 = f32[1,1,128,128]{2,3,1,0:T(8,128)S(1)} custom-call(f32[1,1,128,128]{3,2,1,0:T(8,128)S(1)} %get-tuple-element.32), custom_call_target="InvertDiagBlocksLowerTriangular" | custom-call | tf_op jit(solution)/shard_map/jit(cholesky)/cholesky | solution.py:89
  90.3 0.2 fusion.45
  90.5 0.1 copy.21
  90.6 0.3 fusion.28
  90.9 11.7 %custom-call.18 = f32[1,128,128]{2,1,0:T(8,128)S(1)} custom-call(f32[1,128,128]{2,1,0:T(8,128)S(1)} %fusion.28), custom_call_target="Cholesky" | custom-call | tf_op jit(solution)/shard_map/jit(cholesky)/cholesky | solution.py:89
  102.6 0.1 copy.22
  102.8 0.7 compare_reduce_fusion
  104.8 0.1 triangular_solve.64
  104.9 4.6 %while.1 = (s32[]{:T(128)}, f32[1,256,256]{1,2,0:T(8,128)S(1)}, s32[2,2]{1,0:T(2,128)S(1)}, f32[2,1,128,128]{3,2,1,0:T(8,128)S(1)}, s32[]{:T(128)}) while((s32[]{:T(128)}, f32[1,256,256]{1,2,0:T(8,128)S(1)}, s32[2,2]{1,0:T(2,128)S(1)}, f32[2,1,128,128]{3,2,1,0:T(8,128)S(1)}, s32[]{:T(128)}) %tuple.30), condition=%wide.while_cond, body=%wide.while_body.sunk | while | flops 2 | bytes 393333 | solution.py:91
  105.1 0.7 fusion.85
  105.7 1.4 %constant_dynamic-slice_fusion.5 = f32[1,128,128]{1,2,0:T(8,128)S(1)} fusion(f32[1,256,256]{1,2,0:T(8,128)S(1)} %get-tuple-element.85, s32[]{:T(128)} %bitcast.141, s32[]{:T(128)} %bitcast.142), kind=kLoop, calls=%fused_computation.2.clone.1 | loop fusion | bytes 131080 | tf_op jit(solution)/shard_map/triangular_solve
  107.1 0.1 copy.42
  107.3 0.7 fusion.85
  107.9 1.4 %constant_dynamic-slice_fusion.5 = f32[1,128,128]{1,2,0:T(8,128)S(1)} fusion(f32[1,256,256]{1,2,0:T(8,128)S(1)} %get-tuple-element.85, s32[]{:T(128)} %bitcast.141, s32[]{:T(128)} %bitcast.142), kind=kLoop, calls=%fused_computation.2.clone.1 | loop fusion | bytes 131080 | tf_op jit(solution)/shard_map/triangular_solve
  109.3 0.1 copy.42
  109.5 19.7 %custom-call.19 = f32[1,2,128,128]{2,3,1,0:T(8,128)S(1)} custom-call(f32[1,2,128,128]{3,2,1,0:T(8,128)S(1)} %bitcast.152), custom_call_target="InvertDiagBlocksLowerTriangular" | custom-call | tf_op jit(solution)/shard_map/triangular_solve | solution.py:91
  129.2 0.4 fusion.43
  129.6 0.6 fusion.27
  130.2 0.6 convolution_bitcast_fusion.1
  130.9 1.0 maximum_bitcast_fusion
  (25 shorter events, 0.4 us)
Async XLA Ops:
  0.0 2.5 %copy-start.3 = (bf16[32,8192]{1,0:T(8,128)(2,1)S(1)}, bf16[32,8192]{1,0:T(8,128)(2,1)}, u32[]{:S(2)}) copy-start(bf16[32,8192]{1,0:T(8,128)(2,1)} %param.6) | copy-start | bytes 1572868
  9.8 1.6 %slice-start.1 = ((bf16[5,128,8192]{2,1,0:T(8,128)(2,1)}), bf16[1,128,8192]{2,1,0:T(8,128)(2,1)S(1)}, s32[]{:S(2)}) async-start(bf16[5,128,8192]{2,1,0:T(8,128)(2,1)} %param.8), calls=%async_computation.2 | async-start | bytes 4194304 | tf_op jit(solution)/shard_map/slice | solution.py:30
  9.9 14.8 %collective-permute-start = (f32[4,128,32]{1,2,0:T(8,128)S(1)}, f32[4,128,32]{1,2,0:T(8,128)S(1)}, u32[]{:S(2)}, u32[]{:S(2)}) collective-permute-start(f32[4,128,32]{1,2,0:T(8,128)S(1)} %pad_maximum_fusion), channel_id=1, source_target_pairs={{0,8},{8,0},{16,24},{24,16},{32,40},{40,32},{48,56},{56,48},{64,72... | collective-permute-start | bytes 196616 | tf_op jit(solution)/shard_map/ppermute | solution.py:15
  11.4 2.8 %copy-start.2 = (s32[5]{0:T(128)S(1)}, s32[5]{0:T(128)}, u32[]{:S(2)}) copy-start(s32[5]{0:T(128)} %param.9) | copy-start | bytes 64
  15.5 1.6 %slice-start = ((bf16[5,128,8192]{2,1,0:T(8,128)(2,1)}), bf16[1,128,8192]{2,1,0:T(8,128)(2,1)S(1)}, s32[]{:S(2)}) async-start(bf16[5,128,8192]{2,1,0:T(8,128)(2,1)} %param.7), calls=%async_computation.1 | async-start | bytes 4194304 | tf_op jit(solution)/shard_map/slice | solution.py:69
  19.5 3.7 %copy-start = (bf16[1,128,8192]{1,2,0:T(8,128)(2,1)S(1)}, bf16[1,128,8192]{1,2,0:T(8,128)(2,1)}, u32[]{:S(2)}) copy-start(bf16[1,128,8192]{1,2,0:T(8,128)(2,1)} %copy.29) | copy-start | bytes 6291460
  24.7 6.0 %collective-permute-start.1 = (f32[3,128,32]{1,2,0:T(8,128)S(1)}, f32[3,128,32]{1,2,0:T(8,128)S(1)}, u32[]{:S(2)}, u32[]{:S(2)}) collective-permute-start(f32[3,128,32]{1,2,0:T(8,128)S(1)} %pad_maximum_fusion.1), channel_id=1, source_target_pairs={{0,16},{8,24},{16,0},{24,8},{32,48},{40,56},{48,32},{56,40},{64,80... | collective-permute-start | bytes 147464 | tf_op jit(solution)/shard_map/ppermute | solution.py:15
  30.7 4.0 %collective-permute-start.2 = (f32[2,128,32]{1,2,0:T(8,128)S(1)}, f32[2,128,32]{1,2,0:T(8,128)S(1)}, u32[]{:S(2)}, u32[]{:S(2)}) collective-permute-start(f32[2,128,32]{1,2,0:T(8,128)S(1)} %pad_maximum_fusion.2), channel_id=1, source_target_pairs={{0,32},{8,40},{16,48},{24,56},{32,0},{40,8},{48,16},{56,24},{64,96... | collective-permute-start | bytes 98312 | tf_op jit(solution)/shard_map/ppermute | solution.py:15
  32.1 7.8 %copy-start.1 = (bf16[32,8192]{1,0:T(8,128)(2,1)S(1)}, bf16[32,8192]{1,0:T(8,128)(2,1)}, u32[]{:S(2)}) copy-start(bf16[32,8192]{1,0:T(8,128)(2,1)} %param.5) | copy-start | bytes 1572868
  34.7 5.2 %collective-permute-start.3 = (bf16[1,128,32]{1,2,0:T(8,128)(2,1)S(1)}, bf16[1,128,32]{1,2,0:T(8,128)(2,1)S(1)}, u32[]{:S(2)}, u32[]{:S(2)}) collective-permute-start(bf16[1,128,32]{1,2,0:T(8,128)(2,1)S(1)} %slice_add_fusion), channel_id=1, source_target_pairs={{0,64},{8,72},{16,80},{24,88},{32,96},{40,104},{48,112},{56,120},{... | collective-permute-start | bytes 24584 | tf_op jit(solution)/shard_map/ppermute | solution.py:15
  61.8 6.6 %collective-permute-start.4 = (f32[1,256,256]{1,2,0:T(8,128)S(1)}, f32[1,256,256]{1,2,0:T(8,128)S(1)}, u32[]{:S(2)}, u32[]{:S(2)}) collective-permute-start(f32[1,256,256]{1,2,0:T(8,128)S(1)} %convolution_bitcast_fusion.3), channel_id=1, source_target_pairs={{0,1},{1,0},{2,3},{3,2},{4,5},{5,4},{6,7},{7,6},{8,9},{9,8},{10,11... | collective-permute-start | bytes 786440 | tf_op jit(solution)/shard_map/ppermute | solution.py:15
where the time goes:
time: 132 us
  other arithmetic  58.2 us (44%)
  matrix products  24.1 us (18%)
  blocking collectives  15.4 us (12%)
  local copies, waits for them, and re-layouts  13.9 us (11%)
  waiting for transfers between devices  11.4 us (9%)
  starting transfers between devices  7.13 us (5%)
  between operations  1.64 us (1%)
    another operation x6, other arithmetic, shards(): lower_factor = jnp.linalg.cholesky(shifted)  34 us
    another operation x3, other arithmetic, shards(): lax.linalg.triangular_solve(lower_factor, right_sides, left_side=True, lo...  19.7 us
    all_to_all x1, blocking collectives, shards(): lax.all_to_all(sample, 'probe', split_axis=1, concat_axis=0, tiled=True)  15.4 us
    dot_general x5, matrix products, shards(): jnp.einsum('kcn,rcn->ckr', right_part, probe_part, preferred_element_type...  12.7 us
    ppermute x5, waiting for transfers between devices, from_partner(): return lax.ppermute(value, axis, pairs)  11.4 us
    dot_general x5, matrix products, shards(): jnp.einsum('ckr,kcn->rcn', sibling, left_part, preferred_element_type=jnp...  8.91 us
    ppermute x5, starting transfers between devices, from_partner(): return lax.ppermute(value, axis, pairs)  7.13 us
    another operation x10, local copies, waits for them, and re-layouts  4.31 us
  transfers between devices with their start and end apart: 5, of which 4 were waited for; matrix products, arithmetic and copies ran while one was open for 11% of the time, Pallas kernels for 0%

commit v1 on v0

--- a/solution.py
+++ b/solution.py
@@ -1,12 +1,88 @@
 import jax
 import jax.numpy as jnp
 from jax import lax
+from jax.experimental import pallas as pl
+from jax.experimental.pallas import tpu as pltpu
 from jax.sharding import PartitionSpec as P
 
 BLOCKS = 64
 
 
 ridge_share = 0.05
+
+
+PANEL = 16
+
+
+def split2(x):
+    hi = x.astype(jnp.bfloat16)
+    return hi, (x - hi.astype(jnp.float32)).astype(jnp.bfloat16)
+
+
+def split3(x):
+    hi = x.astype(jnp.bfloat16)
+    rest = x - hi.astype(jnp.float32)
+    mid = rest.astype(jnp.bfloat16)
+    return hi, mid, (rest - mid.astype(jnp.float32)).astype(jnp.bfloat16)
+
+
+def dot32(a, b):
+    return jnp.dot(a, b, preferred_element_type=jnp.float32)
+
+
+def invert_factor(t_ref):
+    size = t_ref.shape[0]
+    m = PANEL
+    sub = lax.broadcasted_iota(jnp.int32, (m, 128), 0)
+    lane = lax.broadcasted_iota(jnp.int32, (m, 128), 1)
+    halves = size // 128
+    for p in range(size // m):
+        j0 = p * m
+        g, jl = j0 // 128, j0 % 128
+        rows = pl.ds(j0, m)
+        panel = [t_ref[rows, pl.ds(128 * h, 128)] for h in range(halves)]
+        diagonal = panel[g]
+        cols = [jnp.broadcast_to(diagonal[:, jl + j : jl + j + 1], (m, 128)) for j in range(m)]
+        inside = (lane >= jl) & (lane < jl + m)
+        panel[g] = jnp.where(inside, jnp.where(lane - jl == sub, 1.0, 0.0), diagonal)
+        outs = [[] for _ in range(halves)]
+        for k in range(m):
+            pivot = jnp.broadcast_to(cols[k][k : k + 1, :], (m, 128))
+            inverse = 1.0 / pivot
+            root = lax.rsqrt(pivot[:1])
+            here = sub == k
+            factor = jnp.where(here, -inverse, cols[k] * inverse)
+            for h in range(halves):
+                row = panel[h][k : k + 1, :]
+                outs[h].append(row * root)
+                panel[h] = jnp.where(here, 0.0, panel[h]) - factor * row
+            for j in range(k + 1, m):
+                row = cols[j][k : k + 1, :]
+                cols[j] = jnp.where(here, 0.0, cols[j]) - factor * row
+        for h in range(halves):
+            t_ref[rows, pl.ds(128 * h, 128)] = jnp.concatenate(outs[h], 0)
+        left = size - j0 - m
+        if left:
+            rest = pl.ds(j0 + m, left)
+            lh, lm, ll = split3(t_ref[rest, pl.ds(128 * g, 128)][:, jl : jl + m])
+            zh, zm, zl = split3(jnp.concatenate(panel, 1))
+            update = dot32(
+                jnp.concatenate([lh, lm, ll, lh, lm, lh], 1),
+                jnp.concatenate([zh, zh, zh, zm, zm, zl], 0),
+            )
+            at = lax.broadcasted_iota(jnp.int32, (left, size), 1)
+            t_ref[rest, :] = jnp.where((at >= j0) & (at < j0 + m), 0.0, t_ref[rest, :]) - update
+
+
+def orthonormalize(gram_ref, sample_ref, basis_ref, work_ref):
+    work_ref[...] = gram_ref[...]
+    invert_factor(work_ref)
+    size = work_ref.shape[0]
+    row_at = lax.broadcasted_iota(jnp.int32, (size, size), 0)
+    col_at = lax.broadcasted_iota(jnp.int32, (size, size), 1)
+    hi, lo = split2(jnp.where(col_at <= row_at, work_ref[...], 0.0))
+    sample = sample_ref[...]
+    basis_ref[...] = dot32(hi, sample) + dot32(lo, sample)
 
 
 def from_partner(value, axis, apart):
@@ -86,10 +162,14 @@
     bit_number = 0
     full_gram = full_gram + from_partner(full_gram, "probe", bit_number)
     shifted = full_gram + ridge_share * block_rows * jnp.eye(all_probes, dtype=jnp.float32)
-    lower_factor = jnp.linalg.cholesky(shifted)
-    right_sides = jnp.transpose(piece_view, (1, 0, 2)).astype(jnp.float32)
-    solved = lax.linalg.triangular_solve(lower_factor, right_sides, left_side=True, lower=True)
-    return jnp.transpose(solved, (1, 0, 2)).reshape(all_probes, slab_rows)
+    return pl.pallas_call(
+        orthonormalize,
+        out_shape=jax.ShapeDtypeStruct(slab.shape, jnp.float32),
+        in_specs=[pl.BlockSpec(memory_space=pltpu.VMEM)] * 2,
+        out_specs=pl.BlockSpec(memory_space=pltpu.VMEM),
+        scratch_shapes=[pltpu.VMEM((all_probes, all_probes), jnp.float32)],
+        name="orthonormalize",
+    )(shifted[0], slab)
 
 
 def solution(mesh):

time: 132 us -> 79.2 us (0.60)
  the two profiles are of different devices: /device:TPU:10 before, /device:TPU:14 now
where the time goes in v1:
time: 79.2 us; the launch traced here: 78.7 us
  matrix products  21.9 us (28%)
  blocking collectives  15.3 us (19%)
  waiting for transfers between devices  12 us (15%)
  Pallas kernels  9.45 us (12%)
  local copies, waits for them, and re-layouts  9.1 us (11%)
  starting transfers between devices  6.54 us (8%)
  other arithmetic  4.2 us (5%)
    all_to_all x1, blocking collectives, shards(): lax.all_to_all(sample, 'probe', split_axis=1, concat_axis=0, tiled=True)  15.3 us
    dot_general x5, matrix products, shards(): jnp.einsum('kcn,rcn->ckr', right_part, probe_part, preferred_element_type...  12.7 us
    ppermute x5, waiting for transfers between devices, from_partner(): return lax.ppermute(value, axis, pairs)  12 us
    pallas_call x1, Pallas kernels, shards(): pl.pallas_call(orthonormalize, out_shape=jax.ShapeDtypeStruct(slab.shape,...  9.45 us
    dot_general x5, matrix products, shards(): jnp.einsum('ckr,kcn->rcn', sibling, left_part, preferred_element_type=jnp...  8.91 us
    ppermute x5, starting transfers between devices, from_partner(): return lax.ppermute(value, axis, pairs)  6.54 us
    lt x5, other arithmetic, shards(): keep_rows = rank_iota[None, :, None] < level_ranks[level_index]  3.4 us
    another operation x1, local copies, waits for them, and re-layouts, shards(): right_factors[level_index]  2.78 us
  transfers between devices with their start and end apart: 5, of which 4 were waited for; matrix products, arithmetic and copies ran while one was open for 19% of the time, Pallas kernels for 0%

profile of v1, /device:TPU:14, one launch (start us, length us, event | category | flops | bytes accessed | tf_op | source)
XLA Modules:
  0.0 78.7 jit_solution(12834302838064549116)
XLA Ops:
  0.0 0.0 copy-start.4
  0.0 2.5 %fusion.26 = f32[1,128,32]{1,2,0:T(8,128)S(1)} fusion(bf16[32,8192]{1,0:T(8,128)(2,1)} %param.6, bf16[5,128,8192]{2,1,0:T(8,128)(2,1)} %param.8), kind=kOutput, calls=%fused_computation.31 | convolution fusion | flops 67108864 | bytes 2637824 | tf_op jit(solution)/shard_map/kcn,rcn->ckr/dot_general | solution.py:111
  2.5 0.0 copy-done.4
  2.6 2.4 %fusion.35 = f32[1,128,32]{1,2,0:T(8,128)S(1)} fusion(bf16[32,8192]{1,0:T(8,128)(2,1)S(1)} %copy-done.4, bf16[5,128,8192]{2,1,0:T(8,128)(2,1)} %param.8), kind=kOutput, calls=%fused_computation.34 | convolution fusion | flops 67108864 | bytes 2637824 | tf_op jit(solution)/shard_map/kcn,rcn->ckr/dot_general | solution.py:111
  5.0 2.4 %fusion.32 = f32[1,128,32]{1,2,0:T(8,128)S(1)} fusion(bf16[32,8192]{1,0:T(8,128)(2,1)S(1)} %copy-done.4, bf16[5,128,8192]{2,1,0:T(8,128)(2,1)} %param.8), kind=kOutput, calls=%fused_computation.33 | convolution fusion | flops 67108864 | bytes 2637824 | tf_op jit(solution)/shard_map/kcn,rcn->ckr/dot_general | solution.py:111
  7.4 2.4 %fusion.29 = f32[1,128,32]{1,2,0:T(8,128)S(1)} fusion(bf16[32,8192]{1,0:T(8,128)(2,1)S(1)} %copy-done.4, bf16[5,128,8192]{2,1,0:T(8,128)(2,1)} %param.8), kind=kOutput, calls=%fused_computation.32 | convolution fusion | flops 67108864 | bytes 2637824 | tf_op jit(solution)/shard_map/kcn,rcn->ckr/dot_general | solution.py:111
  9.8 0.0 slice-start.1
  9.9 0.1 collective-permute-start
  10.0 1.5 %slice-done.1 = bf16[1,128,8192]{2,1,0:T(8,128)(2,1)S(1)} async-done(((bf16[5,128,8192]{2,1,0:T(8,128)(2,1)}), bf16[1,128,8192]{2,1,0:T(8,128)(2,1)S(1)}, s32[]{:S(2)}) %slice-start.1) | async-done | bytes 2097176 | tf_op jit(solution)/shard_map/slice | solution.py:106
  11.4 0.0 copy-start.3
  11.4 2.8 %reshape_squeeze.4 = bf16[128,2,4096]{2,1,0:T(2,128)(2,1)} reshape(bf16[1,128,8192]{2,1,0:T(8,128)(2,1)S(1)} %slice-done.1) | data formatting | bytes 4194304 | tf_op jit(solution)/shard_map/reshape;squeeze | solution.py:106
  14.2 0.0 copy-done.3
  14.2 0.7 fusion.63
  14.9 0.6 iota_compare_fusion.1
  15.5 0.0 slice-start
  15.5 1.6 %slice-done = bf16[1,128,8192]{2,1,0:T(8,128)(2,1)S(1)} async-done(((bf16[5,128,8192]{2,1,0:T(8,128)(2,1)}), bf16[1,128,8192]{2,1,0:T(8,128)(2,1)S(1)}, s32[]{:S(2)}) %slice-start) | async-done | bytes 2097176 | tf_op jit(solution)/shard_map/slice | solution.py:145
  17.1 2.4 %copy.15 = bf16[1,128,8192]{1,2,0:T(8,128)(2,1)} copy(bf16[1,128,8192]{2,1,0:T(8,128)(2,1)S(1)} %slice-done) | data formatting | bytes 4194304
  19.6 0.0 copy-start.1
  19.6 0.8 iota_compare_fusion.4
  20.3 2.9 %fusion.16 = bf16[2,128,32]{1,2,0:T(8,128)(2,1)S(1)} fusion(bf16[128,2,4096]{2,1,0:T(2,128)(2,1)} %reshape_squeeze.4, bf16[4,2,8,4096]{3,2,1,0:T(8,128)(2,1)S(1)} %bitcast.91), kind=kOutput, calls=%fused_computation.20 | convolution fusion | flops 67108864 | bytes 2637824 | tf_op jit(solution)/shard_map/kcn,rcn->ckr/dot_general | solution.py:111
  23.2 0.0 copy-done.1
  23.3 0.8 %convolution_bitcast_fusion = f32[2,4,8,4096]{3,2,1,0:T(8,128)S(1)} fusion(bf16[2,128,32]{1,2,0:T(8,128)(2,1)S(1)} %select_convert_fusion, bf16[128,2,4096]{0,2,1:T(8,128)(2,1)S(1)} %bitcast.87), kind=kOutput, calls=%fused_computation.6 | convolution fusion | flops 67108864 | bytes 3162112 | tf_op jit(solution)/shard_map/ckr,kcn->rcn/dot_general | solution.py:148
  24.1 0.6 iota_compare_fusion.5
  24.7 0.0 collective-permute-done
  24.8 4.0 %collective-permute-start.1 = (f32[3,128,32]{1,2,0:T(8,128)S(1)}, f32[3,128,32]{1,2,0:T(8,128)S(1)}, u32[]{:S(2)}, u32[]{:S(2)}) collective-permute-start(f32[3,128,32]{1,2,0:T(8,128)S(1)} %pad_maximum_fusion.1), channel_id=1, source_target_pairs={{0,16},{8,24},{16,0},{24,8},{32,48},{40,56},{48,32},{56,40},{64,80... | collective-permute-start | bytes 147464 | tf_op jit(solution)/shard_map/ppermute | solution.py:91
  28.7 0.7 iota_compare_fusion.3
  29.4 1.4 %collective-permute-done.1 = f32[3,128,32]{1,2,0:T(8,128)S(1)} collective-permute-done((f32[3,128,32]{1,2,0:T(8,128)S(1)}, f32[3,128,32]{1,2,0:T(8,128)S(1)}, u32[]{:S(2)}, u32[]{:S(2)}) %collective-permute-start.1) | collective-permute-done | bytes 49184 | tf_op jit(solution)/shard_map/ppermute | solution.py:91
  30.8 0.9 %collective-permute-start.2 = (f32[2,128,32]{1,2,0:T(8,128)S(1)}, f32[2,128,32]{1,2,0:T(8,128)S(1)}, u32[]{:S(2)}, u32[]{:S(2)}) collective-permute-start(f32[2,128,32]{1,2,0:T(8,128)S(1)} %pad_maximum_fusion.2), channel_id=1, source_target_pairs={{0,32},{8,40},{16,48},{24,56},{32,0},{40,8},{48,16},{56,24},{64,96... | collective-permute-start | bytes 98312 | tf_op jit(solution)/shard_map/ppermute | solution.py:91
  31.7 0.6 iota_compare_fusion.2
  32.4 0.1 copy.18
  32.4 0.0 copy-start.2
  32.5 2.4 %collective-permute-done.2 = f32[2,128,32]{1,2,0:T(8,128)S(1)} collective-permute-done((f32[2,128,32]{1,2,0:T(8,128)S(1)}, f32[2,128,32]{1,2,0:T(8,128)S(1)}, u32[]{:S(2)}, u32[]{:S(2)}) %collective-permute-start.2) | collective-permute-done | bytes 32800 | tf_op jit(solution)/shard_map/ppermute | solution.py:91
  34.9 1.3 %collective-permute-start.3 = (bf16[1,128,32]{1,2,0:T(8,128)(2,1)S(1)}, bf16[1,128,32]{1,2,0:T(8,128)(2,1)S(1)}, u32[]{:S(2)}, u32[]{:S(2)}) collective-permute-start(bf16[1,128,32]{1,2,0:T(8,128)(2,1)S(1)} %slice_add_fusion), channel_id=1, source_target_pairs={{0,64},{8,72},{16,80},{24,88},{32,96},{40,104},{48,112},{56,120},{... | collective-permute-start | bytes 24584 | tf_op jit(solution)/shard_map/ppermute | solution.py:91
  36.2 2.0 %fusion.5 = f32[32,8192]{1,0:T(8,128)S(1)} fusion(bf16[5,128,8192]{2,1,0:T(8,128)(2,1)} %param.7, f32[2,128,32]{1,2,0:T(8,128)S(1)} %collective-permute-done.2, pred[128]{0:T(512)(128)(4,1)S(1)} %iota_compare_fusion.4), kind=kOutput, calls=%fused_computation.9 | convolution fusion | flops 67112960 | bytes 3154432 | tf_op jit(solution)/shard_map/ckr,kcn->rcn/dot_general | solution.py:148
  38.2 1.8 %collective-permute-done.3 = bf16[1,128,32]{1,2,0:T(8,128)(2,1)S(1)} collective-permute-done((bf16[1,128,32]{1,2,0:T(8,128)(2,1)S(1)}, bf16[1,128,32]{1,2,0:T(8,128)(2,1)S(1)}, u32[]{:S(2)}, u32[]{:S(2)}) %collective-permute-start.3) | collective-permute-done | bytes 8224 | tf_op jit(solution)/shard_map/ppermute | solution.py:91
  40.0 0.0 copy-done.2
  40.0 2.0 %fusion.1 = f32[32,8192]{1,0:T(8,128)S(1)} fusion(f32[32,8192]{1,0:T(8,128)S(1)} %fusion.5, bf16[5,128,8192]{2,1,0:T(8,128)(2,1)} %param.7, bf16[32,8192]{1,0:T(8,128)(2,1)S(1)} %copy-done.2, bf16[1,128,32]{1,2,0:T(8,128)(2,1)S(1)} %collective-permute-done.3, pred[128]{0:T(512)(128)(4,1)S(1)} %iota_compare_fusion.5), kind=kOutput, calls=%fused_computation.4 | convolution fusion | flops 67899392 | bytes 4726912 | tf_op jit(solution)/shard_map/ckr,kcn->rcn/dot_general | solution.py:148
  42.1 2.0 %convolution_subtract_fusion.1 = f32[32,8192]{1,0:T(8,128)S(1)} fusion(f32[32,8192]{1,0:T(8,128)S(1)} %fusion.1, bf16[5,128,8192]{2,1,0:T(8,128)(2,1)} %param.7, f32[3,128,32]{1,2,0:T(8,128)S(1)} %collective-permute-done.1, pred[128]{0:T(512)(128)(4,1)S(1)} %iota_compare_fusion.3), kind=kOutput, calls=%fused_computation.2 | convolution fusion | flops 67375104 | bytes 4203008 | tf_op jit(solution)/shard_map/ckr,kcn->rcn/dot_general | solution.py:148
  44.1 2.0 %fusion.2 = bf16[32,8192]{1,0:T(8,128)(2,1)S(1)} fusion(f32[32,8192]{1,0:T(8,128)S(1)} %bitcast.88, f32[32,8192]{1,0:T(8,128)S(1)} %convolution_subtract_fusion.1, bf16[5,128,8192]{2,1,0:T(8,128)(2,1)} %param.7, f32[4,128,32]{1,2,0:T(8,128)S(1)} %collective-permute-done, pred[128]{0:T(512)(128)(4,1)S(1)} %iota_compare_fusion.2), kind=kOutput, calls=%fused_computation.5 | convolution fusion | flops 67899392 | bytes 4727296 | tf_op jit(solution)/shard_map/ckr,kcn->rcn/dot_general | solution.py:148
  46.2 15.3 %all_to_all.16 = bf16[32,8,1024]{2,0,1:T(8,128)(2,1)S(1)} all-to-all(bf16[32,8,1024]{2,0,1:T(8,128)(2,1)S(1)} %bitcast.90), channel_id=1, replica_groups=mesh['rows'=16,'probe'=8] {'probe'}, dimensions={1} | all-to-all | bytes 1048576 | tf_op jit(solution)/shard_map/all_to_all | solution.py:151
  61.5 0.0 copy-start
  61.5 0.3 convolution_bitcast_fusion.1
  61.8 0.3 collective-permute-start.4
  62.1 6.4 %collective-permute-done.4 = f32[1,256,256]{2,1,0:T(8,128)S(1)} collective-permute-done((f32[1,256,256]{2,1,0:T(8,128)S(1)}, f32[1,256,256]{2,1,0:T(8,128)S(1)}, u32[]{:S(2)}, u32[]{:S(2)}) %collective-permute-start.4) | collective-permute-done | bytes 262176 | tf_op jit(solution)/shard_map/ppermute | solution.py:91
  68.5 0.7 add_bitcast_fusion.gram_ref
  69.2 0.0 copy-done
  69.2 9.4 %orthonormalize.1 = f32[256,1024]{1,0:T(8,128)} custom-call(f32[256,256]{1,0:T(8,128)} %add_bitcast_fusion.gram_ref, bf16[256,1024]{1,0:T(8,128)(2,1)} %bitcast.86), custom_call_target="tpu_custom_call" | custom-call | tf_op jit(solution)/shard_map/orthonormalize/pallas_call | solution.py:165
  (8 shorter events, 0.1 us)
Async XLA Ops:
  0.0 2.5 %copy-start.4 = (bf16[32,8192]{1,0:T(8,128)(2,1)S(1)}, bf16[32,8192]{1,0:T(8,128)(2,1)}, u32[]{:S(2)}) copy-start(bf16[32,8192]{1,0:T(8,128)(2,1)} %param.6) | copy-start | bytes 1572868
  9.8 1.6 %slice-start.1 = ((bf16[5,128,8192]{2,1,0:T(8,128)(2,1)}), bf16[1,128,8192]{2,1,0:T(8,128)(2,1)S(1)}, s32[]{:S(2)}) async-start(bf16[5,128,8192]{2,1,0:T(8,128)(2,1)} %param.8), calls=%async_computation.2 | async-start | bytes 4194304 | tf_op jit(solution)/shard_map/slice | solution.py:106
  9.9 14.9 %collective-permute-start = (f32[4,128,32]{1,2,0:T(8,128)S(1)}, f32[4,128,32]{1,2,0:T(8,128)S(1)}, u32[]{:S(2)}, u32[]{:S(2)}) collective-permute-start(f32[4,128,32]{1,2,0:T(8,128)S(1)} %pad_maximum_fusion), channel_id=1, source_target_pairs={{0,8},{8,0},{16,24},{24,16},{32,40},{40,32},{48,56},{56,48},{64,72... | collective-permute-start | bytes 196616 | tf_op jit(solution)/shard_map/ppermute | solution.py:91
  11.4 2.8 %copy-start.3 = (s32[5]{0:T(128)S(1)}, s32[5]{0:T(128)}, u32[]{:S(2)}) copy-start(s32[5]{0:T(128)} %param.9) | copy-start | bytes 64
  15.5 1.6 %slice-start = ((bf16[5,128,8192]{2,1,0:T(8,128)(2,1)}), bf16[1,128,8192]{2,1,0:T(8,128)(2,1)S(1)}, s32[]{:S(2)}) async-start(bf16[5,128,8192]{2,1,0:T(8,128)(2,1)} %param.7), calls=%async_computation.1 | async-start | bytes 4194304 | tf_op jit(solution)/shard_map/slice | solution.py:145
  19.6 3.7 %copy-start.1 = (bf16[1,128,8192]{1,2,0:T(8,128)(2,1)S(1)}, bf16[1,128,8192]{1,2,0:T(8,128)(2,1)}, u32[]{:S(2)}) copy-start(bf16[1,128,8192]{1,2,0:T(8,128)(2,1)} %copy.15) | copy-start | bytes 6291460
  24.8 6.0 %collective-permute-start.1 = (f32[3,128,32]{1,2,0:T(8,128)S(1)}, f32[3,128,32]{1,2,0:T(8,128)S(1)}, u32[]{:S(2)}, u32[]{:S(2)}) collective-permute-start(f32[3,128,32]{1,2,0:T(8,128)S(1)} %pad_maximum_fusion.1), channel_id=1, source_target_pairs={{0,16},{8,24},{16,0},{24,8},{32,48},{40,56},{48,32},{56,40},{64,80... | collective-permute-start | bytes 147464 | tf_op jit(solution)/shard_map/ppermute | solution.py:91
  30.8 4.1 %collective-permute-start.2 = (f32[2,128,32]{1,2,0:T(8,128)S(1)}, f32[2,128,32]{1,2,0:T(8,128)S(1)}, u32[]{:S(2)}, u32[]{:S(2)}) collective-permute-start(f32[2,128,32]{1,2,0:T(8,128)S(1)} %pad_maximum_fusion.2), channel_id=1, source_target_pairs={{0,32},{8,40},{16,48},{24,56},{32,0},{40,8},{48,16},{56,24},{64,96... | collective-permute-start | bytes 98312 | tf_op jit(solution)/shard_map/ppermute | solution.py:91
  32.4 7.6 %copy-start.2 = (bf16[32,8192]{1,0:T(8,128)(2,1)S(1)}, bf16[32,8192]{1,0:T(8,128)(2,1)}, u32[]{:S(2)}) copy-start(bf16[32,8192]{1,0:T(8,128)(2,1)} %param.5) | copy-start | bytes 1572868
  34.9 5.2 %collective-permute-start.3 = (bf16[1,128,32]{1,2,0:T(8,128)(2,1)S(1)}, bf16[1,128,32]{1,2,0:T(8,128)(2,1)S(1)}, u32[]{:S(2)}, u32[]{:S(2)}) collective-permute-start(bf16[1,128,32]{1,2,0:T(8,128)(2,1)S(1)} %slice_add_fusion), channel_id=1, source_target_pairs={{0,64},{8,72},{16,80},{24,88},{32,96},{40,104},{48,112},{56,120},{... | collective-permute-start | bytes 24584 | tf_op jit(solution)/shard_map/ppermute | solution.py:91
  61.5 7.7 %copy-start = (bf16[32,8,1024]{2,0,1:T(8,128)(2,1)}, bf16[32,8,1024]{2,0,1:T(8,128)(2,1)S(1)}, u32[]{:S(2)}) copy-start(bf16[32,8,1024]{2,0,1:T(8,128)(2,1)S(1)} %all_to_all.16) | copy-start | bytes 1572868
  61.8 6.6 %collective-permute-start.4 = (f32[1,256,256]{2,1,0:T(8,128)S(1)}, f32[1,256,256]{2,1,0:T(8,128)S(1)}, u32[]{:S(2)}, u32[]{:S(2)}) collective-permute-start(f32[1,256,256]{2,1,0:T(8,128)S(1)} %convolution_bitcast_fusion.1), channel_id=1, source_target_pairs={{0,1},{1,0},{2,3},{3,2},{4,5},{5,4},{6,7},{7,6},{8,9},{9,8},{10,11... | collective-permute-start | bytes 786440 | tf_op jit(solution)/shard_map/ppermute | solution.py:91

commit v2 on v1

v2 whole, which is shorter than its diff:
```python
import jax
import jax.numpy as jnp
from jax import lax
from jax.experimental import pallas as pl
from jax.experimental.pallas import tpu as pltpu
from jax.sharding import PartitionSpec as P

BLOCKS = 64


ridge_share = 0.05


PANEL = 16


def split2(x):
    hi = x.astype(jnp.bfloat16)
    return hi, (x - hi.astype(jnp.float32)).astype(jnp.bfloat16)


def split3(x):
    hi = x.astype(jnp.bfloat16)
    rest = x - hi.astype(jnp.float32)
    mid = rest.astype(jnp.bfloat16)
    return hi, mid, (rest - mid.astype(jnp.float32)).astype(jnp.bfloat16)


def dot32(a, b):
    return jnp.dot(a, b, preferred_element_type=jnp.float32)


def invert_factor(t_ref):
    size = t_ref.shape[0]
    m = PANEL
    sub = lax.broadcasted_iota(jnp.int32, (m, 128), 0)
    lane = lax.broadcasted_iota(jnp.int32, (m, 128), 1)
    halves = size // 128
    for p in range(size // m):
        j0 = p * m
        g, jl = j0 // 128, j0 % 128
        rows = pl.ds(j0, m)
        panel = [t_ref[rows, pl.ds(128 * h, 128)] for h in range(halves)]
        diagonal = panel[g]
        cols = [jnp.broadcast_to(diagonal[:, jl + j : jl + j + 1], (m, 128)) for j in range(m)]
        inside = (lane >= jl) & (lane < jl + m)
        panel[g] = jnp.where(inside, jnp.where(lane - jl == sub, 1.0, 0.0), diagonal)
        outs = [[] for _ in range(halves)]
        for k in range(m):
            pivot = jnp.broadcast_to(cols[k][k : k + 1, :], (m, 128))
            inverse = 1.0 / pivot
            root = lax.rsqrt(pivot[:1])
            here = sub == k
            factor = jnp.where(here, -inverse, cols[k] * inverse)
            for h in range(halves):
                row = panel[h][k : k + 1, :]
                outs[h].append(row * root)
                panel[h] = jnp.where(here, 0.0, panel[h]) - factor * row
            for j in range(k + 1, m):
                row = cols[j][k : k + 1, :]
                cols[j] = jnp.where(here, 0.0, cols[j]) - factor * row
        for h in range(halves):
            t_ref[rows, pl.ds(128 * h, 128)] = jnp.concatenate(outs[h], 0)
        left = size - j0 - m
        if left:
            rest = pl.ds(j0 + m, left)
            lh, lm, ll = split3(t_ref[rest, pl.ds(128 * g, 128)][:, jl : jl + m])
            zh, zm, zl = split3(jnp.concatenate(panel, 1))
            update = dot32(
                jnp.concatenate([lh, lm, ll, lh, lm, lh], 1),
                jnp.concatenate([zh, zh, zh, zm, zm, zl], 0),
            )
            at = lax.broadcasted_iota(jnp.int32, (left, size), 1)
            t_ref[rest, :] = jnp.where((at >= j0) & (at < j0 + m), 0.0, t_ref[rest, :]) - update


def orthonormalize(gram_ref, sample_ref, basis_ref, work_ref):
    work_ref[...] = gram_ref[...]
    invert_factor(work_ref)
    size = work_ref.shape[0]
    row_at = lax.broadcasted_iota(jnp.int32, (size, size), 0)
    col_at = lax.broadcasted_iota(jnp.int32, (size, size), 1)
    hi, lo = split2(jnp.where(col_at <= row_at, work_ref[...], 0.0))
    sample = sample_ref[...]
    basis_ref[...] = dot32(hi, sample) + dot32(lo, sample)


MESH = pl.DeviceIdType.MESH
ROWS_AXIS = 16
PROBE_AXIS = 8


def sample_kernel(
    ranks_ref,
    resp_hbm,
    probes_hbm,
    left_hbm,
    right_hbm,
    sample_out,
    gram_out,
    probes_v,
    right_v,
    left_v,
    resp_v,
    sample_v,
    sib_v,
    part_v,
    sum_v,
    near_v,
    far_v,
    last_v,
    local_sem,
    right_sem,
    near_send,
    near_recv,
    far_send,
    far_recv,
    sib_send,
    sib_recv,
    resp_send,
    resp_recv,
):
    r = lax.axis_index("rows")
    p = lax.axis_index("probe")
    core = r % 2
    high = (r // 2) % 2
    x = r // 4
    levels = right_v.shape[0]
    width = right_v.shape[1]
    local = probes_v.shape[0]
    pair_rows = resp_v.shape[1]
    half_rows = pair_rows // 2

    near = []
    for offset in (1, 2, 3):
        other = x * 4 + ((high + offset // 2) % 2) * 2 + (core + offset % 2) % 2
        near.append((other, p))
    in_plane = high * 2 + core
    x_pair = x + 1 - 2 * (x % 2)
    x_far = 2 - 2 * (x // 2)
    far = [(x_pair * 4 + in_plane, p), (x_far * 4 + in_plane, p), ((x_far + 1) * 4 + in_plane, p)]
    group = [(r, (p + d) % PROBE_AXIS) for d in range(1, PROBE_AXIS)]

    barrier = pltpu.get_barrier_semaphore()
    for peer in near + far + group:
        pl.semaphore_signal(barrier, inc=1, device_id=peer, device_id_type=MESH)

    probes_copy = pltpu.make_async_copy(probes_hbm, probes_v, local_sem.at[0])
    probes_copy.start()
    rights = [
        pltpu.make_async_copy(right_hbm.at[l], right_v.at[l], right_sem.at[l]) for l in range(levels)
    ]
    depth = 2
    for l in range(depth):
        rights[l].start()
    pair_at = pl.multiple_of((p // 2) * pair_rows, pair_rows)
    own_rows = pl.ds(pl.multiple_of(p * local, local), local)
    own_resp = pltpu.make_async_copy(
        resp_hbm.at[:, pl.ds(pair_at, pair_rows)], resp_v.at[own_rows, :], local_sem.at[1]
    )
    left_copy = pltpu.make_async_copy(
        left_hbm.at[:, :, pl.ds(pair_at, pair_rows)], left_v, local_sem.at[2]
    )

    lane = lax.broadcasted_iota(jnp.int32, (local, width), 1)

    def coupling(l, start, size):
        value = lax.dot_general(
            probes_v[:, start : start + size],
            right_v[l, :, start : start + size],
            (((1,), (1,)), ((), ())),
            preferred_element_type=jnp.float32,
        )
        return jnp.where(lane < ranks_ref[l], value, 0.0)

    def send(source, target, send_sem, recv_sem, peer):
        copy = pltpu.make_async_remote_copy(
            src_ref=source,
            dst_ref=target,
            send_sem=send_sem,
            recv_sem=recv_sem,
            device_id=peer,
            device_id_type=MESH,
        )
        copy.start()
        return copy

    def ready(l):
        rights[l].wait()
        if l + depth < levels:
            rights[l + depth].start()
        elif l + depth == levels:
            own_resp.start()
            left_copy.start()

    total = probes_v.shape[1]
    started = []
    probes_copy.wait()
    ready(0)
    part_v[0] = coupling(0, 0, total)
    pl.semaphore_wait(barrier, len(near) + len(far) + len(group))

    near_copies = [[None] * 3 for _ in range(4)]
    for i in range(3):
        near_copies[0][i] = send(
            part_v.at[0], near_v.at[0, i], near_send.at[0, i], near_recv.at[0, i], near[i]
        )
    ready(1)
    part_v[1] = coupling(1, 0, total)
    for i in range(3):
        near_copies[1][i] = send(
            part_v.at[1], near_v.at[1, i], near_send.at[1, i], near_recv.at[1, i], near[i]
        )
    ready(2)
    part_v[2] = coupling(2, 0, total)
    for i in (1, 2):
        near_copies[2][i] = send(
            part_v.at[2], near_v.at[2, i], near_send.at[2, i], near_recv.at[2, i], near[i]
        )
    resp_copies = []
    for d, peer in enumerate(group):
        at = pl.multiple_of((peer[1] // 2) * pair_rows, pair_rows)
        resp_copies.append(
            send(
                resp_hbm.at[:, pl.ds(at, pair_rows)],
                resp_v.at[own_rows, :],
                resp_send.at[d],
                resp_recv.at[d],
                peer,
            )
        )

    def block(l):
        return pl.ds(l * width, width)

    def gather(l):
        return [
            send(
                sib_v.at[own_rows, block(l)],
                sib_v.at[own_rows, block(l)],
                sib_send.at[l, d],
                sib_recv.at[l, d],
                peer,
            )
            for d, peer in enumerate(group)
        ]

    for i in range(3):
        near_copies[0][i].wait_recv()
    sum_v[0] = (part_v[0] + near_v[0, 0]) + (near_v[0, 1] + near_v[0, 2])
    far_copies = [
        send(sum_v.at[0], far_v.at[x % 2], far_send.at[i], far_recv.at[x % 2], far[1 + i])
        for i in range(2)
    ]
    ready(3)
    last_v[2] = coupling(3, 0, total).astype(jnp.bfloat16)
    near_copies[3][0] = send(
        last_v.at[2], last_v.at[3], near_send.at[3, 0], near_recv.at[3, 0], near[0]
    )
    for i in range(3):
        near_copies[1][i].wait_recv()
    sum_v[1] = (part_v[1] + near_v[1, 0]) + (near_v[1, 1] + near_v[1, 2])
    pair_copy = send(sum_v.at[1], far_v.at[2], far_send.at[2], far_recv.at[2], far[0])
    ready(4)
    for c in range(2):
        last_v[c] = coupling(4, c * (total // 2), total // 2).astype(jnp.bfloat16)
    gathers = []
    sib_v[own_rows, block(4)] = last_v[1 - p // 4]
    gathers += [
        send(
            last_v.at[1 - peer[1] // 4],
            sib_v.at[own_rows, block(4)],
            sib_send.at[4, d],
            sib_recv.at[4, d],
            peer,
        )
        for d, peer in enumerate(group)
    ]
    for i in (1, 2):
        near_copies[2][i].wait_recv()
    sib_v[own_rows, block(2)] = (near_v[2, 1] + near_v[2, 2]).astype(jnp.bfloat16)
    gathers += gather(2)
    near_copies[3][0].wait_recv()
    sib_v[own_rows, block(3)] = last_v[3]
    gathers += gather(3)
    pair_copy.wait_recv()
    sib_v[own_rows, block(1)] = far_v[2].astype(jnp.bfloat16)
    gathers += gather(1)
    for i in range(2):
        pltpu.make_async_remote_copy(
            src_ref=sum_v.at[0],
            dst_ref=far_v.at[i],
            send_sem=far_send.at[i],
            recv_sem=far_recv.at[i],
            device_id=far[1],
            device_id_type=MESH,
        ).wait_recv()
    sib_v[own_rows, block(0)] = (far_v[0] + far_v[1]).astype(jnp.bfloat16)
    gathers += gather(0)

    own_resp.wait()
    left_copy.wait()
    for copy in resp_copies:
        copy.wait_recv()
    for copy in gathers:
        copy.wait_recv()

    chunk = 512
    for c in range(pair_rows // chunk):
        at = slice(c * chunk, (c + 1) * chunk)
        update = dot32(sib_v[...], left_v[:, :, at].reshape(levels * width, chunk))
        sample_v[:, at] = (resp_v[:, at].astype(jnp.float32) - update).astype(jnp.bfloat16)
    gram = lax.dot_general(
        sample_v[...],
        sample_v[...],
        (((1,), (1,)), ((), ())),
        preferred_element_type=jnp.float32,
    )
    size = gram.shape[0]
    row_at = lax.broadcasted_iota(jnp.int32, (size, size), 0)
    col_at = lax.broadcasted_iota(jnp.int32, (size, size), 1)
    gram_out[...] = gram + jnp.where(row_at == col_at, ridge_share * pair_rows, 0.0)
    half_at = pl.multiple_of((p % 2) * half_rows, half_rows)
    sample_out[...] = sample_v[:, pl.ds(half_at, half_rows)]

    for copies in near_copies:
        for copy in copies:
            if copy is not None:
                copy.wait_send()
    for copy in far_copies + [pair_copy] + resp_copies + gathers:
        copy.wait_send()


def shards(responses, probes, left_factors, right_factors, level_ranks):
    levels, width, rows_dev = right_factors.shape
    local = probes.shape[0]
    probe_count = local * PROBE_AXIS
    block_rows = rows_dev * ROWS_AXIS // BLOCKS
    slab_rows = rows_dev // PROBE_AXIS
    vmem = pl.BlockSpec(memory_space=pltpu.VMEM)
    anywhere = pl.BlockSpec(memory_space=pl.ANY)
    bf16, f32 = jnp.bfloat16, jnp.float32
    dma = pltpu.SemaphoreType.DMA
    sample, gram = pl.pallas_call(
        sample_kernel,
        out_shape=(
            jax.ShapeDtypeStruct((probe_count, slab_rows), bf16),
            jax.ShapeDtypeStruct((probe_count, probe_count), f32),
        ),
        in_specs=[pl.BlockSpec(memory_space=pltpu.SMEM)] + [anywhere] * 4,
        out_specs=(vmem, vmem),
        scratch_shapes=[
            pltpu.VMEM((local, rows_dev), bf16),
            pltpu.VMEM((levels, width, rows_dev), bf16),
            pltpu.VMEM((levels, width, block_rows), bf16),
            pltpu.VMEM((probe_count, block_rows), bf16),
            pltpu.VMEM((probe_count, block_rows), bf16),
            pltpu.VMEM((probe_count, levels * width), bf16),
            pltpu.VMEM((3, local, width), f32),
            pltpu.VMEM((2, local, width), f32),
            pltpu.VMEM((3, 3, local, width), f32),
            pltpu.VMEM((3, local, width), f32),
            pltpu.VMEM((4, local, width), bf16),
            dma((3,)),
            dma((levels,)),
            dma((4, 3)),
            dma((4, 3)),
            dma((3,)),
            dma((3,)),
            dma((levels, PROBE_AXIS - 1)),
            dma((levels, PROBE_AXIS - 1)),
            dma((PROBE_AXIS - 1,)),
            dma((PROBE_AXIS - 1,)),
        ],
        compiler_params=pltpu.CompilerParams(collective_id=0, has_side_effects=True),
        name="sample_and_gram",
    )(level_ranks, responses, probes, left_factors, right_factors)
    return pl.pallas_call(
        orthonormalize,
        out_shape=jax.ShapeDtypeStruct(sample.shape, f32),
        in_specs=[vmem] * 2,
        out_specs=vmem,
        scratch_shapes=[pltpu.VMEM((probe_count, probe_count), f32)],
        name="orthonormalize",
    )(gram, sample)


def solution(mesh):
    return jax.shard_map(
        shards,
        mesh=mesh,
        in_specs=(
            P("probe", "rows"),
            P("probe", "rows"),
            P(None, None, "rows"),
            P(None, None, "rows"),
            P(),
        ),
        out_specs=P(None, ("rows", "probe")),
        check_vma=False,
    )
```

time: 79.2 us -> 41 us (0.52)
  the two profiles are of different devices: /device:TPU:14 before, /device:TPU:1 now
where the time goes in v2:
time: 41 us; the launch traced here: 40.8 us
  Pallas kernels  40.8 us (100%)
    pallas_call x1, Pallas kernels, shards(): pl.pallas_call(sample_kernel, out_shape=(jax.ShapeDtypeStruct((probe_coun...  31.4 us
    pallas_call x1, Pallas kernels, shards(): pl.pallas_call(orthonormalize, out_shape=jax.ShapeDtypeStruct(sample.shap...  9.45 us

profile of v2, /device:TPU:1, one launch (start us, length us, event | category | flops | bytes accessed | tf_op | source)
XLA Modules:
  0.0 40.8 jit_solution(563339149933119589)
XLA Ops:
  0.0 31.4 %sample_and_gram.1 = (bf16[256,1024]{1,0:T(8,128)(2,1)}, f32[256,256]{1,0:T(8,128)}) custom-call(s32[5]{0:T(128)} %ranks_ref.1, bf16[32,8192]{1,0:T(8,128)(2,1)} %resp_hbm.1, bf16[32,8192]{1,0:T(8,128)(2,1)} %probes_hbm.1, bf16[5,128,8192]{2,1,0:T(8,128)(2,1)} %left_hbm.1, bf16[5,128,8192]{2,1,0:T(8,128)(2,1)} %right_hbm.1), custom_call_target="tpu_custom_call" | custom-call | tf_op jit(solution)/shard_map/sample_and_gram/pallas_call | solution.py:344
  31.4 9.4 %orthonormalize.1 = f32[256,1024]{1,0:T(8,128)} custom-call(f32[256,256]{1,0:T(8,128)} %get-tuple-element.7.gram_ref, bf16[256,1024]{1,0:T(8,128)(2,1)} %get-tuple-element.8.sample_ref), custom_call_target="tpu_custom_call" | custom-call | tf_op jit(solution)/shard_map/orthonormalize/pallas_call | solution.py:378

commit v3 on v2

--- a/solution.py
+++ b/solution.py
@@ -88,6 +88,7 @@
 MESH = pl.DeviceIdType.MESH
 ROWS_AXIS = 16
 PROBE_AXIS = 8
+RING = 4
 
 
 def sample_kernel(
@@ -107,7 +108,9 @@
     part_v,
     sum_v,
     near_v,
+    near2_v,
     far_v,
+    stage_v,
     last_v,
     local_sem,
     right_sem,
@@ -117,18 +120,24 @@
     far_recv,
     sib_send,
     sib_recv,
-    resp_send,
-    resp_recv,
+    ring_send,
+    ring_recv,
+    forward_send,
+    forward_recv,
+    cross_send,
+    cross_recv,
 ):
     r = lax.axis_index("rows")
     p = lax.axis_index("probe")
     core = r % 2
     high = (r // 2) % 2
     x = r // 4
+    z = p // RING
+    y = p % RING
     levels = right_v.shape[0]
     width = right_v.shape[1]
     local = probes_v.shape[0]
-    pair_rows = resp_v.shape[1]
+    pair_rows = resp_v.shape[2]
     half_rows = pair_rows // 2
 
     near = []
@@ -140,6 +149,8 @@
     x_far = 2 - 2 * (x // 2)
     far = [(x_pair * 4 + in_plane, p), (x_far * 4 + in_plane, p), ((x_far + 1) * 4 + in_plane, p)]
     group = [(r, (p + d) % PROBE_AXIS) for d in range(1, PROBE_AXIS)]
+    ring = [(r, z * RING + (y + d) % RING) for d in range(1, RING)]
+    across = (r, (1 - z) * RING + y)
 
     barrier = pltpu.get_barrier_semaphore()
     for peer in near + far + group:
@@ -151,16 +162,19 @@
         pltpu.make_async_copy(right_hbm.at[l], right_v.at[l], right_sem.at[l]) for l in range(levels)
     ]
     depth = 2
-    for l in range(depth):
-        rights[l].start()
-    pair_at = pl.multiple_of((p // 2) * pair_rows, pair_rows)
+    rights[0].start()
+
+    def pair_columns(pair):
+        return pl.ds(pl.multiple_of(pair * pair_rows, pair_rows), pair_rows)
+
+    own_pair = y // 2
     own_rows = pl.ds(pl.multiple_of(p * local, local), local)
+    across_rows = pl.ds(pl.multiple_of(across[1] * local, local), local)
+    own_columns = pair_columns(p // 2)
     own_resp = pltpu.make_async_copy(
-        resp_hbm.at[:, pl.ds(pair_at, pair_rows)], resp_v.at[own_rows, :], local_sem.at[1]
+        resp_hbm.at[:, own_columns], resp_v.at[own_pair, own_rows, :], local_sem.at[1]
     )
-    left_copy = pltpu.make_async_copy(
-        left_hbm.at[:, :, pl.ds(pair_at, pair_rows)], left_v, local_sem.at[2]
-    )
+    left_copy = pltpu.make_async_copy(left_hbm.at[:, :, own_columns], left_v, local_sem.at[2])
 
     lane = lax.broadcasted_iota(jnp.int32, (local, width), 1)
 
@@ -187,105 +201,144 @@
 
     def ready(l):
         rights[l].wait()
+        if l == 0:
+            rights[1].start()
         if l + depth < levels:
             rights[l + depth].start()
         elif l + depth == levels:
             own_resp.start()
             left_copy.start()
 
+    def cross(i):
+        half = i % 2
+        pair = (own_pair + 1 + i // 2) % 2
+        columns = pl.ds(
+            pl.multiple_of(((1 - z) * 2 + pair) * pair_rows + half * half_rows, half_rows), half_rows
+        )
+        return send(
+            resp_hbm.at[:, columns],
+            resp_v.at[pair, own_rows, pl.ds(half * half_rows, half_rows)],
+            cross_send.at[i],
+            cross_recv.at[i],
+            across,
+        )
+
     total = probes_v.shape[1]
-    started = []
     probes_copy.wait()
     ready(0)
     part_v[0] = coupling(0, 0, total)
     pl.semaphore_wait(barrier, len(near) + len(far) + len(group))
 
-    near_copies = [[None] * 3 for _ in range(4)]
-    for i in range(3):
-        near_copies[0][i] = send(
-            part_v.at[0], near_v.at[0, i], near_send.at[0, i], near_recv.at[0, i], near[i]
+    near_copies = [
+        send(part_v.at[0], near_v.at[i], near_send.at[0, i], near_recv.at[0, i], near[i])
+        for i in range(3)
+    ]
+    crossing = [cross(0)]
+    ring_copies = []
+    for d, peer in enumerate(ring):
+        pair = (peer[1] % RING) // 2
+        ring_copies.append(
+            send(
+                resp_hbm.at[:, pair_columns(peer[1] // 2)],
+                resp_v.at[pair, own_rows, :],
+                ring_send.at[0, d],
+                ring_recv.at[0, d],
+                peer,
+            )
         )
     ready(1)
     part_v[1] = coupling(1, 0, total)
-    for i in range(3):
-        near_copies[1][i] = send(
-            part_v.at[1], near_v.at[1, i], near_send.at[1, i], near_recv.at[1, i], near[i]
-        )
+    crossing.append(cross(1))
     ready(2)
     part_v[2] = coupling(2, 0, total)
-    for i in (1, 2):
-        near_copies[2][i] = send(
-            part_v.at[2], near_v.at[2, i], near_send.at[2, i], near_recv.at[2, i], near[i]
-        )
-    resp_copies = []
-    for d, peer in enumerate(group):
-        at = pl.multiple_of((peer[1] // 2) * pair_rows, pair_rows)
-        resp_copies.append(
+    near2_copies = [
+        send(
+            part_v.at[pl.ds(1, 2)], near2_v.at[i], near_send.at[1, i], near_recv.at[1, i], near[i]
+        )
+        for i in range(3)
+    ]
+    crossing += [cross(2), cross(3)]
+    ready(3)
+    last_v[0] = coupling(3, 0, total).astype(jnp.bfloat16)
+    core_copy = send(last_v.at[0], last_v.at[1], near_send.at[2, 0], near_recv.at[2, 0], near[0])
+    ready(4)
+    for c in range(2):
+        stage_v[1 - c, :, 2 * width : 3 * width] = coupling(
+            4, c * (total // 2), total // 2
+        ).astype(jnp.bfloat16)
+
+    forwards = []
+
+    def forward_other(half):
+        crossing[half].wait_recv()
+        place = pl.ds(half * half_rows, half_rows)
+        other = (own_pair + 1) % 2
+        for member in range(2):
+            peer = (r, z * RING + other * 2 + member)
+            forwards.append(
+                pltpu.make_async_remote_copy(
+                    src_ref=resp_v.at[other, across_rows, place],
+                    dst_ref=resp_v.at[other, across_rows, place],
+                    send_sem=forward_send.at[half, member],
+                    recv_sem=forward_recv.at[half, y % 2],
+                    device_id=peer,
+                    device_id_type=MESH,
+                )
+            )
+            forwards[-1].start()
+
+    def forward_own(half):
+        crossing[2 + half].wait_recv()
+        place = pl.ds(half * half_rows, half_rows)
+        peer = (r, p + 1 - 2 * (y % 2))
+        forwards.append(
             send(
-                resp_hbm.at[:, pl.ds(at, pair_rows)],
-                resp_v.at[own_rows, :],
-                resp_send.at[d],
-                resp_recv.at[d],
+                resp_v.at[own_pair, across_rows, place],
+                resp_v.at[own_pair, across_rows, place],
+                forward_send.at[half, 2],
+                forward_recv.at[half, 2],
                 peer,
             )
         )
 
-    def block(l):
-        return pl.ds(l * width, width)
-
-    def gather(l):
-        return [
-            send(
-                sib_v.at[own_rows, block(l)],
-                sib_v.at[own_rows, block(l)],
-                sib_send.at[l, d],
-                sib_recv.at[l, d],
-                peer,
-            )
-            for d, peer in enumerate(group)
-        ]
-
-    for i in range(3):
-        near_copies[0][i].wait_recv()
-    sum_v[0] = (part_v[0] + near_v[0, 0]) + (near_v[0, 1] + near_v[0, 2])
+    forward_other(0)
+    forward_other(1)
+    for copy in near_copies:
+        copy.wait_recv()
+    sum_v[0] = (part_v[0] + near_v[0]) + (near_v[1] + near_v[2])
     far_copies = [
         send(sum_v.at[0], far_v.at[x % 2], far_send.at[i], far_recv.at[x % 2], far[1 + i])
         for i in range(2)
     ]
-    ready(3)
-    last_v[2] = coupling(3, 0, total).astype(jnp.bfloat16)
-    near_copies[3][0] = send(
-        last_v.at[2], last_v.at[3], near_send.at[3, 0], near_recv.at[3, 0], near[0]
-    )
-    for i in range(3):
-        near_copies[1][i].wait_recv()
-    sum_v[1] = (part_v[1] + near_v[1, 0]) + (near_v[1, 1] + near_v[1, 2])
+    for copy in near2_copies:
+        copy.wait_recv()
+    sum_v[1] = (part_v[1] + near2_v[0, 0]) + (near2_v[1, 0] + near2_v[2, 0])
     pair_copy = send(sum_v.at[1], far_v.at[2], far_send.at[2], far_recv.at[2], far[0])
-    ready(4)
+    forward_own(0)
+    core_copy.wait_recv()
+    level3 = (near2_v[1, 1] + near2_v[2, 1]).astype(jnp.bfloat16)
     for c in range(2):
-        last_v[c] = coupling(4, c * (total // 2), total // 2).astype(jnp.bfloat16)
-    gathers = []
-    sib_v[own_rows, block(4)] = last_v[1 - p // 4]
-    gathers += [
+        stage_v[c, :, :width] = level3
+        stage_v[c, :, width : 2 * width] = last_v[1]
+
+    def columns_of(first, count):
+        return pl.ds(first * width, count * width)
+
+    gathers = [
         send(
-            last_v.at[1 - peer[1] // 4],
-            sib_v.at[own_rows, block(4)],
-            sib_send.at[4, d],
-            sib_recv.at[4, d],
+            stage_v.at[peer[1] // RING],
+            sib_v.at[own_rows, columns_of(2, 3)],
+            sib_send.at[0, d],
+            sib_recv.at[0, d],
             peer,
         )
         for d, peer in enumerate(group)
     ]
-    for i in (1, 2):
-        near_copies[2][i].wait_recv()
-    sib_v[own_rows, block(2)] = (near_v[2, 1] + near_v[2, 2]).astype(jnp.bfloat16)
-    gathers += gather(2)
-    near_copies[3][0].wait_recv()
-    sib_v[own_rows, block(3)] = last_v[3]
-    gathers += gather(3)
+    sib_v[own_rows, columns_of(2, 3)] = stage_v[z]
+
+    forward_own(1)
     pair_copy.wait_recv()
-    sib_v[own_rows, block(1)] = far_v[2].astype(jnp.bfloat16)
-    gathers += gather(1)
+    sib_v[own_rows, columns_of(1, 1)] = far_v[2].astype(jnp.bfloat16)
     for i in range(2):
         pltpu.make_async_remote_copy(
             src_ref=sum_v.at[0],
@@ -295,21 +348,39 @@
             device_id=far[1],
             device_id_type=MESH,
         ).wait_recv()
-    sib_v[own_rows, block(0)] = (far_v[0] + far_v[1]).astype(jnp.bfloat16)
-    gathers += gather(0)
+    sib_v[own_rows, columns_of(0, 1)] = (far_v[0] + far_v[1]).astype(jnp.bfloat16)
+    gathers += [
+        send(
+            sib_v.at[own_rows, columns_of(0, 2)],
+            sib_v.at[own_rows, columns_of(0, 2)],
+            sib_send.at[1, d],
+            sib_recv.at[1, d],
+            peer,
+        )
+        for d, peer in enumerate(group)
+    ]
 
     own_resp.wait()
     left_copy.wait()
-    for copy in resp_copies:
+    for copy in ring_copies + gathers:
         copy.wait_recv()
-    for copy in gathers:
-        copy.wait_recv()
+    for half in range(2):
+        place = pl.ds(half * half_rows, half_rows)
+        for member in range(3):
+            pltpu.make_async_remote_copy(
+                src_ref=resp_v.at[own_pair, across_rows, place],
+                dst_ref=resp_v.at[own_pair, across_rows, place],
+                send_sem=forward_send.at[half, member],
+                recv_sem=forward_recv.at[half, member],
+                device_id=across,
+                device_id_type=MESH,
+            ).wait_recv()
 
     chunk = 512
     for c in range(pair_rows // chunk):
         at = slice(c * chunk, (c + 1) * chunk)
         update = dot32(sib_v[...], left_v[:, :, at].reshape(levels * width, chunk))
-        sample_v[:, at] = (resp_v[:, at].astype(jnp.float32) - update).astype(jnp.bfloat16)
+        sample_v[:, at] = (resp_v[own_pair, :, at].astype(jnp.float32) - update).astype(jnp.bfloat16)
     gram = lax.dot_general(
         sample_v[...],
         sample_v[...],
@@ -323,11 +394,8 @@
     half_at = pl.multiple_of((p % 2) * half_rows, half_rows)
     sample_out[...] = sample_v[:, pl.ds(half_at, half_rows)]
 
-    for copies in near_copies:
-        for copy in copies:
-            if copy is not None:
-                copy.wait_send()
-    for copy in far_copies + [pair_copy] + resp_copies + gathers:
+    sent = near_copies + near2_copies + [core_copy] + far_copies + [pair_copy]
+    for copy in sent + ring_copies + crossing + forwards + gathers:
         copy.wait_send()
 
 
@@ -353,24 +421,30 @@
             pltpu.VMEM((local, rows_dev), bf16),
             pltpu.VMEM((levels, width, rows_dev), bf16),
             pltpu.VMEM((levels, width, block_rows), bf16),
-            pltpu.VMEM((probe_count, block_rows), bf16),
+            pltpu.VMEM((2, probe_count, block_rows), bf16),
             pltpu.VMEM((probe_count, block_rows), bf16),
             pltpu.VMEM((probe_count, levels * width), bf16),
             pltpu.VMEM((3, local, width), f32),
             pltpu.VMEM((2, local, width), f32),
-            pltpu.VMEM((3, 3, local, width), f32),
             pltpu.VMEM((3, local, width), f32),
-            pltpu.VMEM((4, local, width), bf16),
+            pltpu.VMEM((3, 2, local, width), f32),
+            pltpu.VMEM((3, local, width), f32),
+            pltpu.VMEM((2, local, 3 * width), bf16),
+            pltpu.VMEM((2, local, width), bf16),
             dma((3,)),
             dma((levels,)),
-            dma((4, 3)),
-            dma((4, 3)),
+            dma((3, 3)),
+            dma((3, 3)),
             dma((3,)),
             dma((3,)),
-            dma((levels, PROBE_AXIS - 1)),
-            dma((levels, PROBE_AXIS - 1)),
-            dma((PROBE_AXIS - 1,)),
-            dma((PROBE_AXIS - 1,)),
+            dma((2, PROBE_AXIS - 1)),
+            dma((2, PROBE_AXIS - 1)),
+            dma((1, RING - 1)),
+            dma((1, RING - 1)),
+            dma((2, 3)),
+            dma((2, 3)),
+            dma((4,)),
+            dma((4,)),
         ],
         compiler_params=pltpu.CompilerParams(collective_id=0, has_side_effects=True),
         name="sample_and_gram",

time: 41 us -> 37.5 us (0.915)
  Pallas kernels: 40.8 us -> 37.3 us
    pallas_call x1, Pallas kernels: 31.4 us -> 27.9 us  [shards(): pl.pallas_call(sample_kernel, out_shape=(jax.ShapeDtypeStruct((probe_coun...]
where the time goes in v3:
time: 37.5 us; the launch traced here: 37.3 us
  Pallas kernels  37.3 us (99%)
    pallas_call x1, Pallas kernels, shards(): pl.pallas_call(sample_kernel, out_shape=(jax.ShapeDtypeStruct((probe_coun...  27.9 us
    pallas_call x1, Pallas kernels, shards(): pl.pallas_call(orthonormalize, out_shape=jax.ShapeDtypeStruct(sample.shap...  9.45 us

profile of v3, /device:TPU:1, one launch (start us, length us, event | category | flops | bytes accessed | tf_op | source)
XLA Modules:
  0.0 37.3 jit_solution(18189164774277650343)
XLA Ops:
  0.0 27.9 %sample_and_gram.1 = (bf16[256,1024]{1,0:T(8,128)(2,1)}, f32[256,256]{1,0:T(8,128)}) custom-call(s32[5]{0:T(128)} %ranks_ref.1, bf16[32,8192]{1,0:T(8,128)(2,1)} %resp_hbm.1, bf16[32,8192]{1,0:T(8,128)(2,1)} %probes_hbm.1, bf16[5,128,8192]{2,1,0:T(8,128)(2,1)} %left_hbm.1, bf16[5,128,8192]{2,1,0:T(8,128)(2,1)} %right_hbm.1), custom_call_target="tpu_custom_call" | custom-call | tf_op jit(solution)/shard_map/sample_and_gram/pallas_call | solution.py:412
  27.9 9.4 %orthonormalize.1 = f32[256,1024]{1,0:T(8,128)} custom-call(f32[256,256]{1,0:T(8,128)} %get-tuple-element.7.gram_ref, bf16[256,1024]{1,0:T(8,128)(2,1)} %get-tuple-element.8.sample_ref), custom_call_target="tpu_custom_call" | custom-call | tf_op jit(solution)/shard_map/orthonormalize/pallas_call | solution.py:452
